TPU v7x, 256 devices: a whole 4x4x8 slice. The times are simulated.
256 devices in a mesh: row: 16 (over z, core), col: 8 (over x_hi, y), feat: 2 (over x_lo).
Axes of the slice: x: 4 (x_hi: 2, x_lo: 2; x = x_hi * 2 + x_lo), y: 4, z: 8, core: 2. Of those that a mesh axis runs over, the one named last changes fastest.
Arguments:
- features: bfloat16 [65536, 256], P(('col', 'row'), 'feat'), may hold values from -6 to 6
- tile_rows: int32 [16, 8, 256], P('row', 'col'), may hold values from 0 to 31, as said below
- tile_cols: int32 [16, 8, 256], P('row', 'col'), may hold values from 0 to 63
- tile_count: int32 [16, 8], P('row', 'col'), may hold values from 64 to 256, as said below
- tile_values: bfloat16 [16, 8, 256, 128, 128], P('row', 'col'), may hold values from -0.21875 to 0.21875
- weights: bfloat16 [256, 256], replicated, may hold values from -0.375 to 0.375
- cotangent: bfloat16 [65536, 256], P(('row', 'col'), 'feat'), may hold values from -6 to 6
Outputs:
- activated: bfloat16 [65536, 256], P(('row', 'col'), 'feat')
- feature_grad: bfloat16 [65536, 256], P(('col', 'row'), 'feat')
- weight_grad: float32 [256, 256], P('feat')
Inputs may be any that keep to these rules, and one draw needn't show every extreme that they name: `tile_rows`: block rows of a cell, unevenly loaded. `tile_count`: some cell has all 256 slots live.
All inputs are finite; a program needn't handle non-finite values.
Results may differ from a plain program's by a relative error of at most 0.027.
Values may be sent and summed in bfloat16 or wider, within the bound.
A program may use at most 128 MiB of HBM per device.

v0:
```python
import jax
import jax.numpy as jnp
from jax import lax
from jax.sharding import PartitionSpec as P


def shards(features, tile_rows, tile_cols, tile_count, tile_values, weights, cotangent):
    width = tile_values.shape[-1]
    slots = tile_values.shape[2]
    local_tiles = tile_values[0, 0]
    block_rows = tile_rows[0, 0]
    block_cols = tile_cols[0, 0]
    live_mask = (jnp.arange(slots) < tile_count[0, 0]).astype(jnp.float32)
    n_rowdev = lax.axis_size("row")
    n_coldev = lax.axis_size("col")
    local_blocks = features.shape[0] // width
    feat_half = features.shape[1]
    feat_index = lax.axis_index("feat")
    row_blocks = local_blocks * n_coldev
    col_blocks = local_blocks * n_rowdev
    node_total = features.shape[0] * n_rowdev * n_coldev
    panel = lax.all_gather(features, "row", axis=0, tiled=True)
    gathered = panel.reshape(col_blocks, width, feat_half)[block_cols]
    products = jnp.einsum("tij,tjf->tif", local_tiles, gathered, preferred_element_type=jnp.float32)
    products = products * live_mask[:, None, None]
    partial_value = (
        jnp.zeros((row_blocks, width, feat_half), jnp.float32).at[block_rows].add(products)
    )
    summed = lax.psum_scatter(
        partial_value.reshape(row_blocks * width, feat_half).astype(jnp.bfloat16),
        "col",
        scatter_dimension=0,
        tiled=True,
    )
    weight_rows = lax.dynamic_slice_in_dim(weights, feat_index * feat_half, feat_half, 0)
    mix_term = jnp.dot(summed, weight_rows, preferred_element_type=jnp.float32)
    hidden = lax.psum_scatter(
        mix_term.astype(jnp.bfloat16), "feat", scatter_dimension=1, tiled=True
    ).astype(jnp.float32)
    negative = jnp.minimum(hidden, 0.0)
    activated = jnp.where(hidden > 0, hidden, jnp.expm1(negative)).astype(jnp.bfloat16)
    slope_factor = jnp.where(hidden > 0, 1.0, jnp.exp(negative))
    grad_out = (cotangent.astype(jnp.float32) * slope_factor).astype(jnp.bfloat16)
    grad_whole = lax.all_gather(grad_out, "feat", axis=1, tiled=True)
    weight_term = lax.dot_general(
        summed, grad_whole, (((0,), (0,)), ((), ())), preferred_element_type=jnp.float32
    )
    weight_grad = lax.psum(weight_term, ("row", "col")) * node_total ** (-0.5)
    spread = lax.dot_general(
        grad_whole, weight_rows, (((1,), (1,)), ((), ())), preferred_element_type=jnp.float32
    ).astype(jnp.bfloat16)
    spread_panel = lax.all_gather(spread, "col", axis=0, tiled=True)
    spread_blocks = spread_panel.reshape(row_blocks, width, feat_half)[block_rows]
    back_products = jnp.einsum(
        "tji,tjf->tif", local_tiles, spread_blocks, preferred_element_type=jnp.float32
    )
    back_products = back_products * live_mask[:, None, None]
    back_partial = (
        jnp.zeros((col_blocks, width, feat_half), jnp.float32).at[block_cols].add(back_products)
    )
    back_summed = lax.psum_scatter(
        back_partial.reshape(col_blocks * width, feat_half).astype(jnp.bfloat16),
        "row",
        scatter_dimension=0,
        tiled=True,
    )
    return (activated, back_summed, weight_grad)


def solution(mesh):
    return jax.shard_map(
        shards,
        mesh=mesh,
        in_specs=(
            P(("col", "row"), "feat"),
            P("row", "col", None),
            P("row", "col", None),
            P("row", "col"),
            P("row", "col", None, None, None),
            P(),
            P(("row", "col"), "feat"),
        ),
        out_specs=(P(("row", "col"), "feat"), P(("col", "row"), "feat"), P("feat", None)),
        check_vma=False,
    )
```

profile of v0, /device:TPU:2, one launch (start us, length us, event | category | flops | bytes accessed | tf_op | source)
XLA Modules:
  0.0 1467.3 jit_solution(11761849151452895008)
XLA Ops:
  10.0 42.6 %all-gather.3.cloned.1.call-done = bf16[8192,128]{1,0:T(8,128)(2,1)} async-done(((bf16[512,128]{1,0:T(8,128)(2,1)}), bf16[8192,128]{1,0:T(8,128)(2,1)}) %all-gather.3.cloned.1.call-update) | async-done | bytes 2097168 | tf_op jit(solution)/shard_map/all_gather | solution.py:22
  52.6 10.2 gather_fusion
  62.8 13.0 multiply_bitcast_fusion.1
  75.8 17.5 %copy.17 = f32[256,128,128]{2,1,0:T(8,128)} copy(f32[256,128,128]{1,2,0:T(8,128)} %multiply_bitcast_fusion.1) | data formatting | bytes 33554432 | tf_op jit(solution)/shard_map/mul | solution.py:25
  93.5 33.2 %scatter_fusion = f32[32,128,128]{2,1,0:T(8,128)S(1)} fusion(f32[32,128,128]{2,1,0:T(8,128)S(1)} %broadcast_in_dim.8, s32[256]{0:T(256)S(1)} %bitcast.37, f32[256,128,128]{2,1,0:T(8,128)} %copy.17), kind=kCustom, calls=%fused_computation.2 | custom fusion | flops 4194304 | bytes 50332672 | tf_op jit(solution)/shard_map/scatter-add | solution.py:27
  126.6 1.1 convert_element_type.38
  127.9 74.5 %reduce-scatter.6.cloned.1.call-done = bf16[512,128]{1,0:T(8,128)(2,1)} async-done(((bf16[4096,128]{1,0:T(8,128)(2,1)}), bf16[512,128]{1,0:T(8,128)(2,1)}) %reduce-scatter.6.cloned.1.call-update) | async-done | bytes 131088 | tf_op jit(solution)/shard_map/reduce_scatter | solution.py:29
  202.3 1.1 convolution_convert_fusion
  203.5 0.8 copy.22
  204.4 16.0 %reduce-scatter.10.cloned.1.call-done = bf16[128,512]{1,0:T(8,128)(2,1)} async-done(((bf16[256,512]{1,0:T(8,128)(2,1)}), bf16[128,512]{1,0:T(8,128)(2,1)}) %reduce-scatter.10.cloned.1.call-update) | async-done | bytes 131088
  220.4 1.0 copy.23
  222.2 5.9 all_gather.10
  228.1 0.9 convolution_convert_fusion.1
  229.1 1.8 fusion.12
  231.2 50.7 %all-gather.5.cloned.1.call-done = bf16[4096,128]{1,0:T(8,128)(2,1)} async-done(((bf16[512,128]{1,0:T(8,128)(2,1)}), bf16[4096,128]{1,0:T(8,128)(2,1)}) %all-gather.5.cloned.1.call-update) | async-done | bytes 1048592 | tf_op jit(solution)/shard_map/all_gather | solution.py:52
  281.9 9.8 gather_fusion.1
  291.7 15.4 %multiply_bitcast_fusion = f32[256,128,128]{1,2,0:T(8,128)} fusion(bf16[256,128,128]{2,1,0:T(8,128)(2,1)} %gather_fusion.1, bf16[1,1,256,128,128]{4,3,2,1,0:T(8,128)(2,1)} %param.11, f32[256]{0:T(256)S(1)} %compare_convert_fusion), kind=kOutput, calls=%fused_computation.4 | convolution fusion | flops 1077936128 | bytes 33555456 | tf_op jit(solution)/shard_map/tji,tjf->tif/dot_general | solution.py:54
  307.1 17.4 %copy.19 = f32[256,128,128]{2,1,0:T(8,128)} copy(f32[256,128,128]{1,2,0:T(8,128)} %multiply_bitcast_fusion) | data formatting | bytes 33554432 | tf_op jit(solution)/shard_map/mul | solution.py:57
  324.5 2.4 broadcast_in_dim.9
  327.0 51.9 %scatter_fusion.1 = f32[64,128,128]{2,1,0:T(8,128)} fusion(f32[64,128,128]{2,1,0:T(8,128)} %broadcast_in_dim.9, s32[256]{0:T(256)S(1)} %bitcast.36, f32[256,128,128]{2,1,0:T(8,128)} %copy.19), kind=kCustom, calls=%fused_computation.3 | custom fusion | flops 4194304 | bytes 50332672 | tf_op jit(solution)/shard_map/scatter-add | solution.py:59
  378.8 3.9 convert_element_type.46
  382.8 1018.1 %all-reduce.2.cloned.1.call-done = f32[128,256]{1,0:T(8,128)} async-done(((f32[128,256]{1,0:T(8,128)}), f32[128,256]{1,0:T(8,128)}) %all-reduce.2.cloned.1.call-update) | async-done | bytes 131088 | tf_op jit(solution)/shard_map/psum | solution.py:48
  1400.8 1.6 broadcast_multiply_fusion
  1402.4 58.0 %reduce-scatter.8.cloned.1.call-done = bf16[512,128]{1,0:T(8,128)(2,1)} async-done(((bf16[8192,128]{1,0:T(8,128)(2,1)}), bf16[512,128]{1,0:T(8,128)(2,1)}) %reduce-scatter.8.cloned.1.call-update) | async-done | bytes 131088 | tf_op jit(solution)/shard_map/reduce_scatter | solution.py:61
  (25 shorter events, 3.6 us)
Async XLA Ops:
  7.2 195.2 %copy-start = (bf16[256,256]{1,0:T(8,128)(2,1)S(1)}, bf16[256,256]{1,0:T(8,128)(2,1)}, u32[]{:S(2)}) copy-start(bf16[256,256]{1,0:T(8,128)(2,1)} %param.12) | copy-start | bytes 393220
  7.2 45.4 %all-gather.3.cloned.1.call-start = ((), (), s32[]{:S(2)}) async-start(), calls=%async_computation.3 | async-start | bytes 2228224 | tf_op jit(solution)/shard_map/all_gather | solution.py:22
  7.9 194.4 %reduce-scatter.6.cloned.1.call-start = ((), (), s32[]{:S(2)}) async-start(), calls=%async_computation.4 | async-start | bytes 1179648 | tf_op jit(solution)/shard_map/reduce_scatter | solution.py:29
  93.4 128.0 %copy-start.2 = (bf16[512,128]{1,0:T(8,128)(2,1)S(1)}, bf16[512,128]{1,0:T(8,128)(2,1)}, u32[]{:S(2)}) copy-start(bf16[512,128]{1,0:T(8,128)(2,1)} %param.13) | copy-start | bytes 393220
  127.8 92.6 %reduce-scatter.10.cloned.1.call-start = ((), (), s32[]{:S(2)}) async-start(), calls=%async_computation.8 | async-start | bytes 393216
  204.3 77.5 %all-gather.5.cloned.1.call-start = ((), (), s32[]{:S(2)}) async-start(), calls=%async_computation.5 | async-start | bytes 1179648 | tf_op jit(solution)/shard_map/all_gather | solution.py:52
  229.0 1171.8 %all-reduce.2.cloned.1.call-start = ((), (), s32[]{:S(2)}) async-start(), calls=%async_computation.7 | async-start | bytes 262144 | tf_op jit(solution)/shard_map/psum | solution.py:48
  230.9 1229.5 %reduce-scatter.8.cloned.1.call-start = ((), (), s32[]{:S(2)}) async-start(), calls=%async_computation.6 | async-start | bytes 2228224 | tf_op jit(solution)/shard_map/reduce_scatter | solution.py:61
  327.0 1133.5 %copy-start.1 = (bf16[256,256]{1,0:T(8,128)(2,1)S(1)}, bf16[256,256]{1,0:T(8,128)(2,1)}, u32[]{:S(2)}) copy-start(bf16[256,256]{1,0:T(8,128)(2,1)} %param.12) | copy-start | bytes 393220
Sparse Core Ops, SparseCore 0:
  9.8 42.6 all-gather.2
  127.9 74.3 reduce-scatter.5
  205.0 15.3 reduce-scatter.9
  229.2 52.6 all-gather.4
  284.9 1115.9 all-reduce.1
  1404.0 56.4 reduce-scatter.7
where the time goes:
time: 1470 us
  waiting for transfers between devices  1260 us (86%)
  other arithmetic  93.8 us (6%)
  local copies, waits for them, and re-layouts  59.5 us (4%)
  matrix products  32.2 us (2%)
  between operations  14.8 us (1%)
    psum x1, waiting for transfers between devices, shards(): weight_grad = lax.psum(weight_term, ('row', 'col')) * node_total ** (-0.5)  1020 us
    reduce_scatter x1, waiting for transfers between devices, shards(): lax.psum_scatter(partial_value.reshape(row_blocks * width, feat_half).ast...  74.5 us
    reduce_scatter x1, waiting for transfers between devices, shards(): lax.psum_scatter(back_partial.reshape(col_blocks * width, feat_half).asty...  58 us
    scatter-add x1, other arithmetic, shards(): jnp.zeros((col_blocks, width, feat_half), jnp.float32).at[block_cols]  51.9 us
    all_gather x1, waiting for transfers between devices, shards(): spread_panel = lax.all_gather(spread, 'col', axis=0, tiled=True)  50.7 us
    all_gather x1, waiting for transfers between devices, shards(): panel = lax.all_gather(features, 'row', axis=0, tiled=True)  42.6 us
    scatter-add x1, other arithmetic, shards(): jnp.zeros((row_blocks, width, feat_half), jnp.float32).at[block_rows]  33.2 us
  transfers between devices with their start and end apart: 6, of which 6 were waited for; matrix products, arithmetic and copies ran while one was open for 7% of the time, Pallas kernels for 0%

commit v1 on v0

--- a/solution.py
+++ b/solution.py
@@ -45,7 +45,7 @@
     weight_term = lax.dot_general(
         summed, grad_whole, (((0,), (0,)), ((), ())), preferred_element_type=jnp.float32
     )
-    weight_grad = lax.psum(weight_term, ("row", "col")) * node_total ** (-0.5)
+    weight_grad = lax.psum(lax.psum(weight_term, "row"), "col") * node_total ** (-0.5)
     spread = lax.dot_general(
         grad_whole, weight_rows, (((1,), (1,)), ((), ())), preferred_element_type=jnp.float32
     ).astype(jnp.bfloat16)

time: 1470 us -> 563 us (0.38)
  waiting for transfers between devices: 1260 us -> 354 us
    psum x1 -> x2, waiting for transfers between devices: 1020 us -> 109 us  [the longest x1 109 us: shards(): lax.psum(weight_term, 'row')]
  transfers between devices with their start and end apart: 6 -> 7, of which waited for: 6 -> 6; matrix products, arithmetic and copies ran while one was open for 7% -> 19% of each run, Pallas kernels for 0% -> 0%
where the time goes in v1:
time: 563 us; the launch traced here: 561 us
  waiting for transfers between devices  354 us (63%)
  other arithmetic  93.8 us (17%)
  local copies, waits for them, and re-layouts  59.5 us (11%)
  matrix products  32.2 us (6%)
  between operations  14.9 us (3%)
  blocking collectives  5.89 us (1%)
    psum x1, waiting for transfers between devices, shards(): lax.psum(weight_term, 'row')  109 us
    reduce_scatter x1, waiting for transfers between devices, shards(): lax.psum_scatter(partial_value.reshape(row_blocks * width, feat_half).ast...  74.5 us
    reduce_scatter x1, waiting for transfers between devices, shards(): lax.psum_scatter(back_partial.reshape(col_blocks * width, feat_half).asty...  57.5 us
    all_gather x1, waiting for transfers between devices, shards(): spread_panel = lax.all_gather(spread, 'col', axis=0, tiled=True)  54.1 us
    scatter-add x1, other arithmetic, shards(): jnp.zeros((col_blocks, width, feat_half), jnp.float32).at[block_cols]  51.8 us
    all_gather x1, waiting for transfers between devices, shards(): panel = lax.all_gather(features, 'row', axis=0, tiled=True)  42.6 us
    scatter-add x1, other arithmetic, shards(): jnp.zeros((row_blocks, width, feat_half), jnp.float32).at[block_rows]  33.2 us
    mul x1, local copies, waits for them, and re-layouts, shards(): back_products = back_products * live_mask[:, None, None]  17.5 us
  transfers between devices with their start and end apart: 7, of which 6 were waited for; matrix products, arithmetic and copies ran while one was open for 19% of the time, Pallas kernels for 0%

profile of v1, /device:TPU:2, one launch (start us, length us, event | category | flops | bytes accessed | tf_op | source)
XLA Modules:
  0.0 560.8 jit_solution(3845216165604454085)
XLA Ops:
  10.0 42.6 %all-gather.3.cloned.1.call-done = bf16[8192,128]{1,0:T(8,128)(2,1)} async-done(((bf16[512,128]{1,0:T(8,128)(2,1)}), bf16[8192,128]{1,0:T(8,128)(2,1)}) %all-gather.3.cloned.1.call-update) | async-done | bytes 2097168 | tf_op jit(solution)/shard_map/all_gather | solution.py:22
  52.6 10.2 %gather_fusion = bf16[256,128,128]{2,1,0:T(8,128)(2,1)} fusion(bf16[64,128,128]{2,1,0:T(8,128)(2,1)} %bitcast.30, s32[1024]{0:T(1024)S(1)} %pad_clamp_fusion.1), kind=kCustom, calls=%fused_computation | custom fusion | bytes 16778240 | tf_op jit(solution)/shard_map/gather | solution.py:23
  62.8 13.0 %multiply_bitcast_fusion.1 = f32[256,128,128]{1,2,0:T(8,128)} fusion(bf16[256,128,128]{2,1,0:T(8,128)(2,1)} %gather_fusion, bf16[1,1,256,128,128]{4,3,2,1,0:T(8,128)(2,1)} %param.11, f32[256]{0:T(256)S(1)} %compare_convert_fusion), kind=kOutput, calls=%fused_computation.5 | convolution fusion | flops 1077936128 | bytes 33555456 | tf_op jit(solution)/shard_map/tij,tjf->tif/dot_general | solution.py:24
  75.8 17.5 %copy.17 = f32[256,128,128]{2,1,0:T(8,128)} copy(f32[256,128,128]{1,2,0:T(8,128)} %multiply_bitcast_fusion.1) | data formatting | bytes 33554432 | tf_op jit(solution)/shard_map/mul | solution.py:25
  93.5 33.2 %scatter_fusion = f32[32,128,128]{2,1,0:T(8,128)S(1)} fusion(f32[32,128,128]{2,1,0:T(8,128)S(1)} %broadcast_in_dim.8, s32[256]{0:T(256)S(1)} %bitcast.37, f32[256,128,128]{2,1,0:T(8,128)} %copy.17), kind=kCustom, calls=%fused_computation.2 | custom fusion | flops 4194304 | bytes 50332672 | tf_op jit(solution)/shard_map/scatter-add | solution.py:27
  126.6 1.1 convert_element_type.38
  127.9 74.5 %reduce-scatter.6.cloned.1.call-done = bf16[512,128]{1,0:T(8,128)(2,1)} async-done(((bf16[4096,128]{1,0:T(8,128)(2,1)}), bf16[512,128]{1,0:T(8,128)(2,1)}) %reduce-scatter.6.cloned.1.call-update) | async-done | bytes 131088 | tf_op jit(solution)/shard_map/reduce_scatter | solution.py:29
  202.3 1.1 convolution_convert_fusion
  203.5 0.8 copy.22
  204.4 16.0 %reduce-scatter.10.cloned.1.call-done = bf16[128,512]{1,0:T(8,128)(2,1)} async-done(((bf16[256,512]{1,0:T(8,128)(2,1)}), bf16[128,512]{1,0:T(8,128)(2,1)}) %reduce-scatter.10.cloned.1.call-update) | async-done | bytes 131088
  220.4 1.0 copy.23
  222.2 5.9 %all_gather.10 = bf16[512,256]{1,0:T(8,128)(2,1)S(1)} all-gather(bf16[512,128]{1,0:T(8,128)(2,1)S(1)} %get-tuple-element.3), channel_id=1, replica_groups=mesh['row'=16,'col'=8,'feat'=2] {'feat'}, dimensions={1}, use_global_device_ids=true | all-gather | bytes 393216 | tf_op jit(solution)/shard_map/all_gather | solution.py:44
  228.1 1.8 fusion.12
  230.0 0.9 convolution_convert_fusion.1
  231.0 108.6 %all-reduce.3.cloned.1.call-done = f32[128,256]{1,0:T(8,128)} async-done(((f32[128,256]{1,0:T(8,128)}), f32[128,256]{1,0:T(8,128)}) %all-reduce.3.cloned.1.call-update) | async-done | bytes 131088 | tf_op jit(solution)/shard_map/psum | solution.py:48
  339.9 54.1 %all-gather.5.cloned.1.call-done = bf16[4096,128]{1,0:T(8,128)(2,1)} async-done(((bf16[512,128]{1,0:T(8,128)(2,1)}), bf16[4096,128]{1,0:T(8,128)(2,1)}) %all-gather.5.cloned.1.call-update) | async-done | bytes 1048592 | tf_op jit(solution)/shard_map/all_gather | solution.py:52
  394.0 9.8 %gather_fusion.1 = bf16[256,128,128]{2,1,0:T(8,128)(2,1)} fusion(bf16[32,128,128]{2,1,0:T(8,128)(2,1)} %bitcast.29, s32[1024]{0:T(1024)S(1)} %pad_clamp_fusion), kind=kCustom, calls=%fused_computation.1 | custom fusion | bytes 16778240 | tf_op jit(solution)/shard_map/gather | solution.py:53
  403.8 15.4 %multiply_bitcast_fusion = f32[256,128,128]{1,2,0:T(8,128)} fusion(bf16[256,128,128]{2,1,0:T(8,128)(2,1)} %gather_fusion.1, bf16[1,1,256,128,128]{4,3,2,1,0:T(8,128)(2,1)} %param.11, f32[256]{0:T(256)S(1)} %compare_convert_fusion), kind=kOutput, calls=%fused_computation.4 | convolution fusion | flops 1077936128 | bytes 33555456 | tf_op jit(solution)/shard_map/tji,tjf->tif/dot_general | solution.py:54
  419.2 17.5 %copy.19 = f32[256,128,128]{2,1,0:T(8,128)} copy(f32[256,128,128]{1,2,0:T(8,128)} %multiply_bitcast_fusion) | data formatting | bytes 33554432 | tf_op jit(solution)/shard_map/mul | solution.py:57
  436.7 2.4 broadcast_in_dim.9
  439.1 51.8 %scatter_fusion.1 = f32[64,128,128]{2,1,0:T(8,128)} fusion(f32[64,128,128]{2,1,0:T(8,128)} %broadcast_in_dim.9, s32[256]{0:T(256)S(1)} %bitcast.36, f32[256,128,128]{2,1,0:T(8,128)} %copy.19), kind=kCustom, calls=%fused_computation.3 | custom fusion | flops 4194304 | bytes 50332672 | tf_op jit(solution)/shard_map/scatter-add | solution.py:59
  491.0 3.9 convert_element_type.46
  494.9 1.6 broadcast_multiply_fusion
  496.5 57.5 %reduce-scatter.8.cloned.1.call-done = bf16[512,128]{1,0:T(8,128)(2,1)} async-done(((bf16[8192,128]{1,0:T(8,128)(2,1)}), bf16[512,128]{1,0:T(8,128)(2,1)}) %reduce-scatter.8.cloned.1.call-update) | async-done | bytes 131088 | tf_op jit(solution)/shard_map/reduce_scatter | solution.py:61
  (28 shorter events, 3.7 us)
Async XLA Ops:
  7.2 195.2 %copy-start = (bf16[256,256]{1,0:T(8,128)(2,1)S(1)}, bf16[256,256]{1,0:T(8,128)(2,1)}, u32[]{:S(2)}) copy-start(bf16[256,256]{1,0:T(8,128)(2,1)} %param.12) | copy-start | bytes 393220
  7.2 45.4 %all-gather.3.cloned.1.call-start = ((), (), s32[]{:S(2)}) async-start(), calls=%async_computation.3 | async-start | bytes 2228224 | tf_op jit(solution)/shard_map/all_gather | solution.py:22
  7.9 194.4 %reduce-scatter.6.cloned.1.call-start = ((), (), s32[]{:S(2)}) async-start(), calls=%async_computation.4 | async-start | bytes 1179648 | tf_op jit(solution)/shard_map/reduce_scatter | solution.py:29
  93.4 128.0 %copy-start.2 = (bf16[512,128]{1,0:T(8,128)(2,1)S(1)}, bf16[512,128]{1,0:T(8,128)(2,1)}, u32[]{:S(2)}) copy-start(bf16[512,128]{1,0:T(8,128)(2,1)} %param.13) | copy-start | bytes 393220
  127.8 92.6 %reduce-scatter.10.cloned.1.call-start = ((), (), s32[]{:S(2)}) async-start(), calls=%async_computation.9 | async-start | bytes 393216
  204.3 135.3 %all-reduce.3.cloned.1.call-start = ((), (), s32[]{:S(2)}) async-start(), calls=%async_computation.7 | async-start | bytes 262144 | tf_op jit(solution)/shard_map/psum | solution.py:48
  229.9 164.1 %all-gather.5.cloned.1.call-start = ((), (), s32[]{:S(2)}) async-start(), calls=%async_computation.5 | async-start | bytes 1179648 | tf_op jit(solution)/shard_map/all_gather | solution.py:52
  230.9 264.0 %all-reduce.5.cloned.1.call-start = ((), (), s32[]{:S(2)}) async-start(), calls=%async_computation.8 | async-start | bytes 262144 | tf_op jit(solution)/shard_map/psum | solution.py:48
  339.6 214.3 %reduce-scatter.8.cloned.1.call-start = ((), (), s32[]{:S(2)}) async-start(), calls=%async_computation.6 | async-start | bytes 2228224 | tf_op jit(solution)/shard_map/reduce_scatter | solution.py:61
  439.1 114.8 %copy-start.1 = (bf16[256,256]{1,0:T(8,128)(2,1)S(1)}, bf16[256,256]{1,0:T(8,128)(2,1)}, u32[]{:S(2)}) copy-start(bf16[256,256]{1,0:T(8,128)(2,1)} %param.12) | copy-start | bytes 393220
Sparse Core Ops, SparseCore 0:
  9.8 42.6 all-gather.2
  127.9 74.3 reduce-scatter.5
  205.0 15.3 reduce-scatter.9
  230.1 109.5 all-reduce.2
  343.0 50.9 all-gather.4
  396.6 87.8 all-reduce.4
  495.0 58.8 reduce-scatter.7
